TPU v7x, 32 devices: a whole 2x2x4 slice. The times are simulated.
32 devices in a mesh: img: 8 (over z, y), ori: 4 (over x, core).
Axes of the slice: x: 2, y: 2, z: 4, core: 2. Of those that a mesh axis runs over, the one named last changes fastest.
Arguments:
- images: bfloat16 [8192, 4096], P('img'), may hold values from -34 to 34
- img_scale: float32 [8192], P('img'), may hold values from 0.5 to 2
- references: bfloat16 [2048, 4096], P('ori', 'img'), may hold values from -4 to 4
- pattern: int32 [8192, 8], P('img', 'ori'), may hold values from 0 to 1, as said below
- tile_owner: int32 [4, 16384, 1], P('ori', 'img'), may hold values from 0 to 7; in each aligned block of 2048 rows (0 to 2047, 2048 to 4095, ..., all dimensions but the last counted through in order) at most 768 rows name the same one
- tile_brick: int32 [4, 16384], P('ori', 'img'), may hold values from 0 to 15
- tile_block: int32 [4, 16384], P('ori', 'img'), may hold values from 0 to 7
- distance_weights: bfloat16 [8, 128, 512], replicated, may hold values from -0.0234375 to 0.0234375
Outputs:
- bricks: float32 [128, 512], P(('img', 'ori'))
- log_evidence: float32 [8192], P('img')
Inputs may be any that keep to these rules, and one draw needn't show every extreme that they name: `pattern`: each image has at least one orientation group set. `tile_owner`: among the 2048 tiles of each aligned block, at most 768 name the same owner, and some block reaches 768.
All inputs are finite; a program needn't handle non-finite values.
Results may differ from a plain program's by a relative error of at most 0.002.
Values may be sent and summed in bfloat16 or wider, within the bound.
A program may use at most 128 MiB of HBM per device.

v0:
```python
import functools
import math

import jax
import jax.numpy as jnp
from jax import lax
from jax.experimental import pallas as pl
from jax.experimental.pallas import tpu as pltpu
from jax.sharding import PartitionSpec as P

BRICK_DEV = 16
LANES = 128
NY = 2
PARTS = 2
MESH = pl.DeviceIdType.MESH


def plain_body(
    images, img_scale, references, pattern, tile_owner, tile_brick, tile_block, distance_weights
):
    image_rows, width = images.shape
    ref_local = references.shape[0]
    group_size = ref_local // pattern.shape[1]
    positions, tile_width, voxels = distance_weights.shape
    inv_root = 1.0 / math.sqrt(width)
    weight_table = distance_weights.astype(jnp.float32)
    raw_scores = lax.dot_general(
        images,
        lax.all_gather(references, "img", axis=1, tiled=True),
        (((1,), (1,)), ((), ())),
        preferred_element_type=jnp.float32,
    )
    scores = raw_scores * img_scale[:, None] * inv_root
    active = jnp.repeat(pattern > 0, group_size, axis=1)
    masked = jnp.where(active, scores, -1e30)
    local_peak = jnp.max(masked, axis=1)
    peak = lax.pmax(local_peak, "ori")
    expo = jnp.where(active, jnp.exp(masked - peak[:, None]), 0.0)
    mass = lax.psum(jnp.sum(expo, axis=1), "ori")
    weights = expo / mass[:, None]
    log_evidence = peak + jnp.log(mass)
    scaled = (weights * img_scale[:, None]).astype(jnp.bfloat16)
    partial_value = lax.dot_general(
        scaled, images, (((0,), (0,)), ((), ())), preferred_element_type=jnp.float32
    )
    owners = tile_owner.reshape(-1)
    local_code = tile_brick.reshape(-1) * positions + tile_block.reshape(-1)
    cells = BRICK_DEV * positions
    tile_code = owners * cells + local_code
    group_code = lax.all_gather(tile_code, "img", axis=0, tiled=True)
    peers = lax.axis_size("img")
    group_tiles = partial_value.reshape(-1, tile_width)
    collected = jax.ops.segment_sum(group_tiles, group_code, num_segments=peers * cells)
    brick_terms = jnp.einsum(
        "bpt,ptv->bv",
        collected.reshape(peers * BRICK_DEV, positions, tile_width),
        weight_table,
        precision=lax.Precision.HIGHEST,
    )
    bricks = lax.psum_scatter(brick_terms, ("img", "ori"), scatter_dimension=0, tiled=True)
    return (bricks, log_evidence)


def kernel(
    n_img, n_ori, tiles_ref, inv_root,
    refs, images, scale, pattern, owner, brick_of, block_of, weights,
    sums_out, stats_out,
    img_v, buf, w_v, sc, scaled, codes, codes_buf, codes_all, onehot, rhs, rhs_b, acc,
    halves, stats, stats_buf, terms, terms_buf, mid, mid_buf,
    img_sem, w_sem, own_sem, up_sem, dn_sem, y_sem, recv_sem, code_send, code_recv,
    stat_send, stat_recv, a_send, a_recv, b_send, b_recv,
):
    nz = n_img // NY
    me = lax.axis_index("img")
    ori = lax.axis_index("ori")
    z, y = me // NY, me % NY
    zp = z + 1 - 2 * (z % 2)
    rows, depth = refs.shape
    half = rows // 2
    quarter = rows // PARTS
    n_images = img_v.shape[1]
    groups = pattern.shape[0]
    group = rows // groups
    positions, tile_width, voxels = w_v.shape
    chunk_tiles = depth // tile_width
    cells = acc.shape[0]

    def image_copy(f):
        return pltpu.make_async_copy(
            images.at[:, pl.ds(f * depth, depth)], img_v.at[f], img_sem.at[f]
        )

    for f in range(n_img):
        image_copy(f).start()
    w_copy = pltpu.make_async_copy(weights, w_v, w_sem)
    w_copy.start()

    own_copy = pltpu.make_async_copy(refs, buf.at[me], own_sem)
    own_copy.start()

    barrier = pltpu.get_barrier_semaphore()
    for step in range(1, n_img):
        pl.semaphore_signal(
            barrier, inc=1, device_id=((me + step) % n_img, ori), device_id_type=MESH
        )
    for step in range(1, n_ori):
        pl.semaphore_signal(
            barrier, inc=1, device_id=(me, (ori + step) % n_ori), device_id_type=MESH
        )
    per = rows // n_img
    th = tiles_ref // 2
    lines = BRICK_DEV // n_ori
    brick_ids = brick_of[...]
    raw = (
        block_of[...] * (n_img * BRICK_DEV)
        + (brick_ids // lines) * (n_img * lines)
        + owner[...] * lines
        + brick_ids % lines
    )
    held_rows = raw.shape[0]
    turned = jnp.concatenate(
        [raw, jnp.zeros((LANES - held_rows, LANES), jnp.int32)], axis=0
    ).T
    local = jnp.zeros((tiles_ref, LANES), jnp.int32)
    for j in range(LANES // tiles_ref):
        cut = turned[j * tiles_ref:(j + 1) * tiles_ref, :]
        local += pltpu.roll(cut, j * held_rows, 1) if j else cut
    codes[...] = local[0:th, :] + pltpu.roll(local[th:, :], per, 1)

    pl.semaphore_wait(barrier, n_img + n_ori - 2)

    def code_copy(step):
        return pltpu.make_async_remote_copy(
            src_ref=codes,
            dst_ref=codes_buf.at[me],
            send_sem=code_send.at[step],
            recv_sem=code_recv.at[me],
            device_id=((me + step) % n_img, ori),
            device_id_type=MESH,
        )

    def code_arrival(step):
        other = (me + step) % n_img
        return pltpu.make_async_remote_copy(
            src_ref=codes,
            dst_ref=codes_buf.at[other],
            send_sem=code_send.at[step],
            recv_sem=code_recv.at[other],
            device_id=(other, ori),
            device_id_type=MESH,
        )

    def piece(src, sl, q, sems, to):
        return pltpu.make_async_remote_copy(
            src_ref=src,
            dst_ref=buf.at[sl, pl.ds(pl.multiple_of(q * quarter, quarter), quarter), :],
            send_sem=sems.at[sl * PARTS + q],
            recv_sem=recv_sem.at[sl * PARTS + q],
            device_id=(to, ori),
            device_id_type=MESH,
        )

    def held(sl, q):
        return buf.at[sl, pl.ds(pl.multiple_of(q * quarter, quarter), quarter), :]

    up, dn, yn = me + NY, me - NY, z * NY + 1 - y
    has_up, has_dn = z < nz - 1, z > 0

    for step in range(1, n_img):
        code_copy(step).start()
    for h in range(PARTS):
        own = refs.at[pl.ds(h * quarter, quarter), :]

        @pl.when(has_up)
        def _():
            piece(own, me, h, up_sem, up).start()

        @pl.when(has_dn)
        def _():
            piece(own, me, h, dn_sem, dn).start()

        piece(own, me, h, y_sem, yn).start()

    codes_buf[me] = codes[...]
    sc[...] = jnp.zeros_like(sc)
    acc[...] = jnp.zeros_like(acc)
    own_copy.wait()
    for f in range(n_img):
        image_copy(f).wait()
    for step in range(1, n_img):
        code_arrival(step).wait_recv()

    low = lax.broadcasted_iota(jnp.int32, (th, LANES), 1) < per
    for j in range(n_img // 2):
        a, b = codes_buf[2 * j], codes_buf[2 * j + 1]
        codes_all[0:th, j * LANES:(j + 1) * LANES] = jnp.where(low, a, pltpu.roll(b, per, 1))
        codes_all[th:, j * LANES:(j + 1) * LANES] = jnp.where(low, pltpu.roll(a, per, 1), b)

    def place(s):
        r, q, k = s // (4 * PARTS), (s // 4) % PARTS, s % 4
        far = q >= PARTS // 2
        other = k // 2
        dist = r - other
        below = (k % 2) == 0
        slz = jnp.where(below, z - dist, z + dist)
        late = jnp.logical_and(jnp.logical_and(r == nz, far), k == 1)
        ok = jnp.logical_and(slz >= 0, slz < nz)
        ok = jnp.logical_and(ok, dist >= jnp.where(below, 0, 1))
        ok = jnp.logical_and(ok, dist < nz)
        skipped = jnp.logical_and(slz == zp, far)
        ok = jnp.logical_and(
            ok, jnp.logical_not(jnp.logical_and(other == 1, skipped))
        )
        ok = jnp.logical_or(ok, late)
        slz = jnp.where(late, zp, slz)
        sl = jnp.where(jnp.logical_or(other == 1, late), slz * NY + 1 - y, slz * NY + y)
        moving = jnp.logical_and(jnp.logical_and(other == 0, r > 0), jnp.logical_not(late))
        moving = jnp.logical_and(moving, ok)
        go_up = jnp.logical_and(jnp.logical_and(moving, below), has_up)
        go_dn = jnp.logical_and(jnp.logical_and(moving, jnp.logical_not(below)), has_dn)
        go_y = jnp.logical_and(moving, jnp.logical_not(skipped))
        sl = jnp.where(ok, sl, me)
        return r, q, k, sl, ok, go_up, go_dn, go_y

    steps = (nz + 1) * 4 * PARTS
    late_sl = z * NY + 1 - y

    strip = 16
    n_strips = half // strip
    factor = scale[...] * inv_root

    blocks = n_images // LANES

    def score_rows(at):
        return jnp.concatenate([sc[c, at, :] for c in range(blocks)], axis=1)

    def keep_rows(at, value):
        for c in range(blocks):
            sc[c, at, :] = value[:, c * LANES:(c + 1) * LANES]

    def half_softmax(h):
        def at_strip(i):
            i = h * n_strips + i
            flag = pattern[pl.ds(i // (group // strip), 1), :] > 0
            return pl.ds(pl.multiple_of(i * strip, strip), strip), flag

        def peak_of(i, m):
            at, flag = at_strip(i)
            s = jnp.where(flag, score_rows(at) * factor, -1e30)
            keep_rows(at, s)
            return jnp.maximum(m, s)

        m = lax.fori_loop(
            0, n_strips, peak_of, jnp.full((strip, n_images), -1e30, jnp.float32)
        )
        m = jnp.max(m, axis=0, keepdims=True)

        def mass_of(i, t):
            at, flag = at_strip(i)
            e = jnp.where(flag, jnp.exp(score_rows(at) - m), 0.0)
            keep_rows(at, e)
            return t + e

        t = lax.fori_loop(0, n_strips, mass_of, jnp.zeros((strip, n_images), jnp.float32))
        halves[2 * h:2 * h + 1, :] = m
        halves[2 * h + 1:2 * h + 2, :] = jnp.sum(t, axis=0, keepdims=True)

    def arrive(s, carry):
        r, q, k, sl, ok, go_up, go_dn, go_y = place(s)

        @pl.when(s == (nz * PARTS + PARTS // 2) * 4)
        def _():
            half_softmax(0)

        @pl.when(jnp.logical_and(ok, r + k > 0))
        def _():
            piece(held(sl, q), sl, q, y_sem, yn).wait_recv()

        @pl.when(go_up)
        def _():
            piece(held(sl, q), sl, q, up_sem, up).start()

        @pl.when(go_dn)
        def _():
            piece(held(sl, q), sl, q, dn_sem, dn).start()

        @pl.when(go_y)
        def _():
            piece(held(sl, q), sl, q, y_sem, yn).start()

        turn = jnp.logical_and(r == nz - 1, jnp.logical_and(q == 0, k == 0))

        @pl.when(jnp.logical_and(turn, zp > z))
        def _():
            for late_q in range(PARTS // 2, PARTS):
                piece(held(late_sl, late_q), late_sl, late_q, up_sem, up).start()

        @pl.when(jnp.logical_and(turn, zp < z))
        def _():
            for late_q in range(PARTS // 2, PARTS):
                piece(held(late_sl, late_q), late_sl, late_q, dn_sem, dn).start()

        @pl.when(jnp.logical_and(ok, (q + 1) % (PARTS // 2) == 0))
        def _():
            at = pl.ds(pl.multiple_of((q // (PARTS // 2)) * half, half), half)
            term = lax.dot_general(
                buf[sl, at, :], img_v[sl], (((1,), (1,)), ((), ())),
                preferred_element_type=jnp.float32,
            )
            for c in range(blocks):
                sc[c, at, :] += term[:, c * LANES:(c + 1) * LANES]

        @pl.when(s < tiles_ref)
        def _():
            code = codes_all[pl.ds(s, 1), :]
            f, q = s // chunk_tiles, s % chunk_tiles
            at = pl.ds(pl.multiple_of(q * rows, rows), rows)

            def part(i, c):
                base = pl.multiple_of(i * 64, 64)
                row = lax.broadcasted_iota(jnp.int32, (64, rows), 0) + base
                onehot[f, pl.ds(base, 64), at] = jnp.where(row == code, 1.0, 0.0).astype(
                    jnp.bfloat16
                )
                return c

            lax.fori_loop(0, cells // 64, part, 0)

        return carry

    lax.fori_loop(0, steps, arrive, 0)

    half_softmax(1)
    m = jnp.maximum(halves[0:1, :], halves[2:3, :])
    total = halves[1:2, :] * jnp.exp(halves[0:1, :] - m)
    total += halves[3:4, :] * jnp.exp(halves[2:3, :] - m)
    stats[0:1, :] = m
    stats[1:2, :] = total

    def stat_copy(step, slot):
        return pltpu.make_async_remote_copy(
            src_ref=stats,
            dst_ref=stats_buf.at[slot],
            send_sem=stat_send.at[step],
            recv_sem=stat_recv.at[slot],
            device_id=(me, (ori + step) % n_ori),
            device_id_type=MESH,
        )

    for step in range(1, n_ori):
        stat_copy(step, ori).start()
    peak = m
    for step in range(1, n_ori):
        slot = (ori + step) % n_ori
        stat_copy(step, slot).wait_recv()
        peak = jnp.maximum(peak, stats_buf[slot, 0:1, :])
    mass = total * jnp.exp(m - peak)
    for step in range(1, n_ori):
        slot = (ori + step) % n_ori
        mass += stats_buf[slot, 1:2, :] * jnp.exp(stats_buf[slot, 0:1, :] - peak)
    stats_out[0:1, :] = peak
    stats_out[1:2, :] = mass
    share_of = scale[...] / mass

    spread = LANES // tiles_ref
    for h in range(2):
        weight = jnp.exp(halves[2 * h:2 * h + 1, :] - peak) * share_of

        def scale_of(i, c):
            i = h * n_strips + i
            first = (i // spread) * per + i % spread
            at = pl.ds(pl.multiple_of(i * strip, strip), strip)
            scaled[at, :] = (score_rows(pl.ds(first, strip, stride=spread)) * weight).astype(
                jnp.bfloat16
            )
            return c

        lax.fori_loop(0, n_strips, scale_of, 0)

    def values(f, out):
        value = jnp.dot(scaled[...], img_v[f], preferred_element_type=jnp.float32)
        hi = value.astype(jnp.bfloat16)
        lo = (value - hi.astype(jnp.float32)).astype(jnp.bfloat16)
        for q in range(chunk_tiles):
            cut = slice(q * tile_width, (q + 1) * tile_width)
            out[q * rows:(q + 1) * rows, 0:tile_width] = hi[:, cut]
            out[q * rows:(q + 1) * rows, tile_width:] = lo[:, cut]

    def collect(f, tiles):
        acc[...] += jnp.dot(onehot[f], tiles[...], preferred_element_type=jnp.float32)

    values(0, rhs)

    def pair(j, c):
        values(2 * j + 1, rhs_b)
        collect(2 * j, rhs)
        values(2 * j + 2, rhs)
        collect(2 * j + 1, rhs_b)
        return c

    lax.fori_loop(0, n_img // 2 - 1, pair, 0)
    values(n_img - 1, rhs_b)
    collect(n_img - 2, rhs)
    collect(n_img - 1, rhs_b)

    w_copy.wait()
    per_block = cells // positions
    brick = jnp.zeros((per_block, voxels), jnp.float32)
    for p in range(positions):
        cut = slice(p * per_block, (p + 1) * per_block)
        c = acc[cut, 0:tile_width] + acc[cut, tile_width:]
        hi = c.astype(jnp.bfloat16)
        lo = (c - hi.astype(jnp.float32)).astype(jnp.bfloat16)
        brick += jnp.dot(hi, w_v[p], preferred_element_type=jnp.float32)
        brick += jnp.dot(lo, w_v[p], preferred_element_type=jnp.float32)
    share = per_block // n_ori
    for o in range(n_ori):
        terms[o] = brick[o * share:(o + 1) * share, :]

    def term_copy(step, slot):
        to = (ori + step) % n_ori
        return pltpu.make_async_remote_copy(
            src_ref=terms.at[to],
            dst_ref=terms_buf.at[slot],
            send_sem=a_send.at[step],
            recv_sem=a_recv.at[slot],
            device_id=(me, to),
            device_id_type=MESH,
        )

    for step in range(1, n_ori):
        term_copy(step, ori).start()
    mine = terms[ori]
    for step in range(1, n_ori):
        slot = (ori + step) % n_ori
        term_copy(step, slot).wait_recv()
        mine += terms_buf[slot]
    for i in range(n_img):
        mid[i] = mine[i * lines:(i + 1) * lines, :]

    def mid_copy(step, slot):
        to = (me + step) % n_img
        return pltpu.make_async_remote_copy(
            src_ref=mid.at[to],
            dst_ref=mid_buf.at[slot],
            send_sem=b_send.at[step],
            recv_sem=b_recv.at[slot],
            device_id=(to, ori),
            device_id_type=MESH,
        )

    for step in range(1, n_img):
        mid_copy(step, me).start()
    result = mid[me]
    for step in range(1, n_img):
        slot = (me + step) % n_img
        mid_copy(step, slot).wait_recv()
        if step < n_img - 1:
            result += mid_buf[slot]
    sums_out[0] = result
    sums_out[1] = mid_buf[(me + n_img - 1) % n_img]

    for step in range(1, n_img):
        code_copy(step).wait_send()
        mid_copy(step, me).wait_send()
    for step in range(1, n_ori):
        stat_copy(step, ori).wait_send()
        term_copy(step, ori).wait_send()
    for h in range(PARTS):
        own = refs.at[pl.ds(h * quarter, quarter), :]

        @pl.when(has_up)
        def _():
            piece(own, me, h, up_sem, up).wait_send()

        @pl.when(has_dn)
        def _():
            piece(own, me, h, dn_sem, dn).wait_send()

        piece(own, me, h, y_sem, yn).wait_send()

    @pl.when(zp > z)
    def _():
        for late_q in range(PARTS // 2, PARTS):
            piece(held(late_sl, late_q), late_sl, late_q, up_sem, up).wait_send()

    @pl.when(zp < z)
    def _():
        for late_q in range(PARTS // 2, PARTS):
            piece(held(late_sl, late_q), late_sl, late_q, dn_sem, dn).wait_send()

    def drain(s, carry):
        r, q, k, sl, ok, go_up, go_dn, go_y = place(s)

        @pl.when(go_up)
        def _():
            piece(held(sl, q), sl, q, up_sem, up).wait_send()

        @pl.when(go_dn)
        def _():
            piece(held(sl, q), sl, q, dn_sem, dn).wait_send()

        @pl.when(go_y)
        def _():
            piece(held(sl, q), sl, q, y_sem, yn).wait_send()

        return carry

    lax.fori_loop(0, steps, drain, 0)


def finish(sums, stats, bricks, evidence):
    bricks[...] = sums[0] + sums[1]
    evidence[...] = stats[0:1, :] + jnp.log(stats[1:2, :])


def fused_body(
    images, img_scale, references, pattern, tile_owner, tile_brick, tile_block, distance_weights
):
    n_img, n_ori = lax.axis_size("img"), lax.axis_size("ori")
    n_images, width = images.shape
    rows, depth = references.shape
    positions, tile_width, voxels = distance_weights.shape
    tiles_ref = width // tile_width
    lines = BRICK_DEV // n_ori
    cells = n_img * BRICK_DEV * positions
    flat = (tile_brick.size // LANES, LANES)
    bf16, f32, i32 = jnp.bfloat16, jnp.float32, jnp.int32
    vmem = pl.BlockSpec(memory_space=pltpu.VMEM)
    hbm = pl.BlockSpec(memory_space=pl.ANY)
    dma = pltpu.SemaphoreType.DMA
    sums, stats = pl.pallas_call(
        functools.partial(kernel, n_img, n_ori, tiles_ref, 1.0 / math.sqrt(width)),
        out_shape=(
            jax.ShapeDtypeStruct((2, lines, voxels), f32),
            jax.ShapeDtypeStruct((2, n_images), f32),
        ),
        in_specs=[hbm, hbm, vmem, vmem, vmem, vmem, vmem, hbm],
        out_specs=(vmem, vmem),
        scratch_shapes=[
            pltpu.VMEM((n_img, n_images, depth), bf16),
            pltpu.VMEM((n_img, rows, depth), bf16),
            pltpu.VMEM((positions, tile_width, voxels), bf16),
            pltpu.VMEM((n_images // LANES, rows, LANES), f32),
            pltpu.VMEM((rows, n_images), bf16),
            pltpu.VMEM((tiles_ref // 2, LANES), i32),
            pltpu.VMEM((n_img, tiles_ref // 2, LANES), i32),
            pltpu.VMEM((tiles_ref, rows), i32),
            pltpu.VMEM((n_img, cells, rows * depth // tile_width), bf16),
            pltpu.VMEM((rows * depth // tile_width, 2 * tile_width), bf16),
            pltpu.VMEM((rows * depth // tile_width, 2 * tile_width), bf16),
            pltpu.VMEM((cells, 2 * tile_width), f32),
            pltpu.VMEM((4, n_images), f32),
            pltpu.VMEM((2, n_images), f32),
            pltpu.VMEM((n_ori, 2, n_images), f32),
            pltpu.VMEM((n_ori, n_img * lines, voxels), f32),
            pltpu.VMEM((n_ori, n_img * lines, voxels), f32),
            pltpu.VMEM((n_img, lines, voxels), f32),
            pltpu.VMEM((n_img, lines, voxels), f32),
            dma((n_img,)),
            dma,
            dma,
            dma((PARTS * n_img,)),
            dma((PARTS * n_img,)),
            dma((PARTS * n_img,)),
            dma((PARTS * n_img,)),
            dma((n_img,)),
            dma((n_img,)),
            dma((n_ori,)),
            dma((n_ori,)),
            dma((n_ori,)),
            dma((n_ori,)),
            dma((n_img,)),
            dma((n_img,)),
        ],
        compiler_params=pltpu.CompilerParams(
            collective_id=0, has_side_effects=True, vmem_limit_bytes=67043328
        ),
    )(
        references,
        images,
        img_scale[None, :],
        pattern.T,
        tile_owner.reshape(flat),
        tile_brick.reshape(flat),
        tile_block.reshape(flat),
        distance_weights,
    )
    bricks, evidence = pl.pallas_call(
        finish,
        out_shape=(
            jax.ShapeDtypeStruct((lines, voxels), f32),
            jax.ShapeDtypeStruct((1, n_images), f32),
        ),
        in_specs=[vmem, vmem],
        out_specs=(vmem, vmem),
    )(sums, stats)
    return bricks, evidence.reshape(-1)


def body(*args):
    images, references, weights = args[0], args[2], args[7]
    n_img = lax.axis_size("img")
    rows, depth = references.shape
    cells = n_img * BRICK_DEV * weights.shape[0]
    tiles_ref = images.shape[1] // weights.shape[1]
    room = 2 * (images.size + rows * depth * n_img * (1 + cells // weights.shape[1]))
    fits = (
        depth % LANES == 0
        and 2 * (rows // n_img) == LANES
        and LANES % tiles_ref == 0
        and rows * tiles_ref == 16 * LANES * n_img
        and n_img % (2 * NY) == 0
        and n_img >= 4 * NY
        and room < 48 * 2**20
    )
    return fused_body(*args) if fits else plain_body(*args)


def solution(mesh):
    placed = (
        P("img", None),
        P("img"),
        P("ori", "img"),
        P("img", "ori"),
        P("ori", "img", None),
        P("ori", "img"),
        P("ori", "img"),
        P(),
    )
    return jax.shard_map(
        body,
        mesh=mesh,
        in_specs=placed,
        out_specs=(P(("img", "ori"), None), P("img")),
        check_vma=False,
    )
```

profile of v0, /device:TPU:0, one launch (start us, length us, event | category | flops | bytes accessed | tf_op | source)
XLA Modules:
  0.0 83.2 jit_solution(18266556659883697300)
XLA Ops:
  0.6 81.2 %shard_map.95 = (f32[2,4,512]{2,1,0:T(4,128)}, f32[2,1024]{1,0:T(2,128)}) custom-call(bf16[512,512]{1,0:T(8,128)(2,1)} %refs.1, bf16[1024,4096]{1,0:T(8,128)(2,1)} %images.1, f32[1,1024]{1,0:T(1,128)} %bitcast.10, s32[2,1024]{1,0:T(2,128)} %bitcast.6, s32[16,128]{1,0:T(8,128)} %bitcast.7, s32[16,128]{1,0:T(8,128)} %bitcast.8, s32[16,128]{1,0:T(8,128)} %bitcast.9, ...), custom_call_target="tpu_custom_call" | custom-call | tf_op jit(solution)/shard_map/pallas_call | solution.py:532
  81.8 1.3 %shard_map.96 = (f32[4,512]{1,0:T(4,128)}, f32[1,1024]{1,0:T(1,128)}) custom-call(f32[2,4,512]{2,1,0:T(4,128)} %get-tuple-element.6.sums, f32[2,1024]{1,0:T(2,128)} %get-tuple-element.7.stats), custom_call_target="tpu_custom_call" | custom-call | tf_op jit(solution)/shard_map/pallas_call | solution.py:589
where the time goes:
time: 83.5 us; the launch traced here: 83.2 us
  Pallas kernels  82.5 us (99%)
    pallas_call x1, Pallas kernels, fused_body(): pl.pallas_call(functools.partial(kernel, n_img, n_ori, tiles_ref, 1.0 / m...  81.2 us

commit v1 on v0

--- a/solution.py
+++ b/solution.py
@@ -12,6 +12,11 @@
 LANES = 128
 NY = 2
 PARTS = 2
+CORES = 2
+PACK = 1 << 16
+F8 = jnp.float8_e4m3fn
+TOP = 256.0
+LOW = 32.0
 MESH = pl.DeviceIdType.MESH
 
 
@@ -65,10 +70,10 @@
     n_img, n_ori, tiles_ref, inv_root,
     refs, images, scale, pattern, owner, brick_of, block_of, weights,
     sums_out, stats_out,
-    img_v, buf, w_v, sc, scaled, codes, codes_buf, codes_all, onehot, rhs, rhs_b, acc,
+    img_v, buf, w_v, sc, scaled, codes, codes_buf, codes_all, onehot, rhs, acc,
     halves, stats, stats_buf, terms, terms_buf, mid, mid_buf,
     img_sem, w_sem, own_sem, up_sem, dn_sem, y_sem, recv_sem, code_send, code_recv,
-    stat_send, stat_recv, a_send, a_recv, b_send, b_recv,
+    stat_send, stat_recv, a_send, a_recv, b_send, b_recv, hop_sem,
 ):
     nz = n_img // NY
     me = lax.axis_index("img")
@@ -81,7 +86,8 @@
     n_images = img_v.shape[1]
     groups = pattern.shape[0]
     group = rows // groups
-    positions, tile_width, voxels = w_v.shape
+    tile_width, (depth_w, voxels) = acc.shape[1] // 2, w_v.shape
+    positions = depth_w // tile_width
     chunk_tiles = depth // tile_width
     cells = acc.shape[0]
 
@@ -98,11 +104,23 @@
     own_copy = pltpu.make_async_copy(refs, buf.at[me], own_sem)
     own_copy.start()
 
+    up, dn, yn = me + NY, me - NY, z * NY + 1 - y
+    has_up, has_dn = z < nz - 1, z > 0
+    near = 1 + has_up.astype(jnp.int32) + has_dn.astype(jnp.int32)
+
+    def greet(sem):
+        @pl.when(has_up)
+        def _():
+            pl.semaphore_signal(sem, inc=1, device_id=(up, ori), device_id_type=MESH)
+
+        @pl.when(has_dn)
+        def _():
+            pl.semaphore_signal(sem, inc=1, device_id=(dn, ori), device_id_type=MESH)
+
+        pl.semaphore_signal(sem, inc=1, device_id=(yn, ori), device_id_type=MESH)
+
     barrier = pltpu.get_barrier_semaphore()
-    for step in range(1, n_img):
-        pl.semaphore_signal(
-            barrier, inc=1, device_id=((me + step) % n_img, ori), device_id_type=MESH
-        )
+    greet(barrier)
     for step in range(1, n_ori):
         pl.semaphore_signal(
             barrier, inc=1, device_id=(me, (ori + step) % n_ori), device_id_type=MESH
@@ -111,9 +129,11 @@
     th = tiles_ref // 2
     lines = BRICK_DEV // n_ori
     brick_ids = brick_of[...]
+    place_of = brick_ids // lines
     raw = (
-        block_of[...] * (n_img * BRICK_DEV)
-        + (brick_ids // lines) * (n_img * lines)
+        (place_of // CORES) * (cells // (n_ori // CORES))
+        + block_of[...] * (CORES * n_img * lines)
+        + (place_of % CORES) * (n_img * lines)
         + owner[...] * lines
         + brick_ids % lines
     )
@@ -125,9 +145,10 @@
     for j in range(LANES // tiles_ref):
         cut = turned[j * tiles_ref:(j + 1) * tiles_ref, :]
         local += pltpu.roll(cut, j * held_rows, 1) if j else cut
-    codes[...] = local[0:th, :] + pltpu.roll(local[th:, :], per, 1)
-
-    pl.semaphore_wait(barrier, n_img + n_ori - 2)
+    wide = local[0:th, :] + pltpu.roll(local[th:, :], per, 1)
+    codes[...] = wide[0:th // 2, :] + wide[th // 2:, :] * PACK
+
+    pl.semaphore_wait(barrier, near + n_ori - 1)
 
     def code_copy(step):
         return pltpu.make_async_remote_copy(
@@ -163,23 +184,24 @@
     def held(sl, q):
         return buf.at[sl, pl.ds(pl.multiple_of(q * quarter, quarter), quarter), :]
 
-    up, dn, yn = me + NY, me - NY, z * NY + 1 - y
-    has_up, has_dn = z < nz - 1, z > 0
-
+    for h in range(PARTS):
+        own = refs.at[pl.ds(h * quarter, quarter), :]
+
+        @pl.when(has_up)
+        def _():
+            piece(own, me, h, up_sem, up).start()
+
+        @pl.when(has_dn)
+        def _():
+            piece(own, me, h, dn_sem, dn).start()
+
+        piece(own, me, h, y_sem, yn).start()
+
+    for hop in range(nz - 1):
+        greet(hop_sem.at[hop])
+        pl.semaphore_wait(hop_sem.at[hop], near)
     for step in range(1, n_img):
         code_copy(step).start()
-    for h in range(PARTS):
-        own = refs.at[pl.ds(h * quarter, quarter), :]
-
-        @pl.when(has_up)
-        def _():
-            piece(own, me, h, up_sem, up).start()
-
-        @pl.when(has_dn)
-        def _():
-            piece(own, me, h, dn_sem, dn).start()
-
-        piece(own, me, h, y_sem, yn).start()
 
     codes_buf[me] = codes[...]
     sc[...] = jnp.zeros_like(sc)
@@ -187,14 +209,30 @@
     own_copy.wait()
     for f in range(n_img):
         image_copy(f).wait()
-    for step in range(1, n_img):
-        code_arrival(step).wait_recv()
-
-    low = lax.broadcasted_iota(jnp.int32, (th, LANES), 1) < per
-    for j in range(n_img // 2):
-        a, b = codes_buf[2 * j], codes_buf[2 * j + 1]
-        codes_all[0:th, j * LANES:(j + 1) * LANES] = jnp.where(low, a, pltpu.roll(b, per, 1))
-        codes_all[th:, j * LANES:(j + 1) * LANES] = jnp.where(low, pltpu.roll(a, per, 1), b)
+
+    def brightest(i, top):
+        f, at = i // (n_images // 16), pl.multiple_of((i % (n_images // 16)) * 16, 16)
+        return jnp.maximum(top, jnp.abs(img_v[f, pl.ds(at, 16), :]))
+
+    bright = lax.fori_loop(
+        0, n_img * n_images // 16, brightest, jnp.zeros((16, depth), jnp.bfloat16)
+    )
+    bright = jnp.max(bright.astype(jnp.float32), axis=(0, 1), keepdims=True)
+
+    def spread_codes():
+        for step in range(1, n_img):
+            code_arrival(step).wait_recv()
+        low = lax.broadcasted_iota(jnp.int32, (th, LANES), 1) < per
+
+        def unpacked(i):
+            two = codes_buf[i]
+            return jnp.concatenate([two % PACK, two // PACK], axis=0)
+
+        for j in range(n_img // 2):
+            a, b = unpacked(2 * j), unpacked(2 * j + 1)
+            cut = slice(j * LANES, (j + 1) * LANES)
+            codes_all[0:th, cut] = jnp.where(low, a, pltpu.roll(b, per, 1))
+            codes_all[th:, cut] = jnp.where(low, pltpu.roll(a, per, 1), b)
 
     def place(s):
         r, q, k = s // (4 * PARTS), (s // 4) % PARTS, s % 4
@@ -265,12 +303,18 @@
         halves[2 * h:2 * h + 1, :] = m
         halves[2 * h + 1:2 * h + 2, :] = jnp.sum(t, axis=0, keepdims=True)
 
+    first_hot = 2 * 4 * PARTS
+
     def arrive(s, carry):
         r, q, k, sl, ok, go_up, go_dn, go_y = place(s)
 
         @pl.when(s == (nz * PARTS + PARTS // 2) * 4)
         def _():
             half_softmax(0)
+
+        @pl.when(s == first_hot)
+        def _():
+            spread_codes()
 
         @pl.when(jnp.logical_and(ok, r + k > 0))
         def _():
@@ -310,21 +354,23 @@
             for c in range(blocks):
                 sc[c, at, :] += term[:, c * LANES:(c + 1) * LANES]
 
-        @pl.when(s < tiles_ref)
-        def _():
-            code = codes_all[pl.ds(s, 1), :]
-            f, q = s // chunk_tiles, s % chunk_tiles
-            at = pl.ds(pl.multiple_of(q * rows, rows), rows)
-
-            def part(i, c):
-                base = pl.multiple_of(i * 64, 64)
-                row = lax.broadcasted_iota(jnp.int32, (64, rows), 0) + base
-                onehot[f, pl.ds(base, 64), at] = jnp.where(row == code, 1.0, 0.0).astype(
-                    jnp.bfloat16
-                )
-                return c
-
-            lax.fori_loop(0, cells // 64, part, 0)
+        @pl.when(jnp.logical_and(s >= first_hot, s < first_hot + tiles_ref // 2))
+        def _():
+            for u in range(2):
+                tile = 2 * (s - first_hot) + u
+                code = codes_all[pl.ds(tile, 1), :]
+                f, q = tile // chunk_tiles, tile % chunk_tiles
+                at = pl.ds(pl.multiple_of(q * rows, rows), rows)
+
+                def part(i, c):
+                    base = pl.multiple_of(i * 64, 64)
+                    row = lax.broadcasted_iota(jnp.int32, (64, rows), 0) + base
+                    onehot[f, pl.ds(base, 64), at] = jnp.where(row == code, 1.0, 0.0).astype(
+                        F8
+                    )
+                    return c
+
+                lax.fori_loop(0, cells // 64, part, 0)
 
         return carry
 
@@ -363,77 +409,93 @@
     share_of = scale[...] / mass
 
     spread = LANES // tiles_ref
+    power = jnp.zeros((strip, 1), jnp.float32)
     for h in range(2):
         weight = jnp.exp(halves[2 * h:2 * h + 1, :] - peak) * share_of
 
-        def scale_of(i, c):
+        def scale_of(i, top):
             i = h * n_strips + i
             first = (i // spread) * per + i % spread
             at = pl.ds(pl.multiple_of(i * strip, strip), strip)
-            scaled[at, :] = (score_rows(pl.ds(first, strip, stride=spread)) * weight).astype(
-                jnp.bfloat16
-            )
-            return c
-
-        lax.fori_loop(0, n_strips, scale_of, 0)
-
-    def values(f, out):
-        value = jnp.dot(scaled[...], img_v[f], preferred_element_type=jnp.float32)
-        hi = value.astype(jnp.bfloat16)
-        lo = (value - hi.astype(jnp.float32)).astype(jnp.bfloat16)
+            value = score_rows(pl.ds(first, strip, stride=spread)) * weight
+            scaled[at, :] = value.astype(jnp.bfloat16)
+            return jnp.maximum(top, jnp.sum(value * value, axis=1, keepdims=True))
+
+        power = lax.fori_loop(0, n_strips, scale_of, power)
+    largest = jnp.maximum(jnp.sqrt(jnp.max(power, axis=0, keepdims=True)), 1e-15)
+    largest = largest * (math.sqrt(n_images) * jnp.maximum(bright, 1e-18))
+    grow, shrink = TOP / largest, largest * (1.0 / TOP)
+
+    def values(f):
+        value = jnp.dot(scaled[...], img_v[f], preferred_element_type=jnp.float32) * grow
+        hi = value.astype(F8)
+        lo = ((value - hi.astype(jnp.float32)) * LOW).astype(F8)
         for q in range(chunk_tiles):
             cut = slice(q * tile_width, (q + 1) * tile_width)
-            out[q * rows:(q + 1) * rows, 0:tile_width] = hi[:, cut]
-            out[q * rows:(q + 1) * rows, tile_width:] = lo[:, cut]
-
-    def collect(f, tiles):
-        acc[...] += jnp.dot(onehot[f], tiles[...], preferred_element_type=jnp.float32)
-
-    values(0, rhs)
-
-    def pair(j, c):
-        values(2 * j + 1, rhs_b)
-        collect(2 * j, rhs)
-        values(2 * j + 2, rhs)
-        collect(2 * j + 1, rhs_b)
-        return c
-
-    lax.fori_loop(0, n_img // 2 - 1, pair, 0)
-    values(n_img - 1, rhs_b)
-    collect(n_img - 2, rhs)
-    collect(n_img - 1, rhs_b)
-
-    w_copy.wait()
-    per_block = cells // positions
-    brick = jnp.zeros((per_block, voxels), jnp.float32)
-    for p in range(positions):
-        cut = slice(p * per_block, (p + 1) * per_block)
-        c = acc[cut, 0:tile_width] + acc[cut, tile_width:]
+            rhs[f, q * rows:(q + 1) * rows, 0:tile_width] = hi[:, cut]
+            rhs[f, q * rows:(q + 1) * rows, tile_width:] = lo[:, cut]
+
+    x_me, core = ori // CORES, ori % CORES
+    chips = n_ori // CORES
+    side = cells // chips
+    share = n_img * lines
+
+    def collect(f, chip):
+        at = pl.ds(pl.multiple_of(chip * side, side), side)
+        acc[at, :] += jnp.dot(onehot[f, at, :], rhs[f], preferred_element_type=jnp.float32)
+
+    def brick_terms(chip):
+        at = pl.ds(pl.multiple_of(chip * side, side), side)
+        both = acc[at, :]
+        c = (both[:, 0:tile_width] + both[:, tile_width:] * (1.0 / LOW)) * shrink
         hi = c.astype(jnp.bfloat16)
         lo = (c - hi.astype(jnp.float32)).astype(jnp.bfloat16)
-        brick += jnp.dot(hi, w_v[p], preferred_element_type=jnp.float32)
-        brick += jnp.dot(lo, w_v[p], preferred_element_type=jnp.float32)
-    share = per_block // n_ori
-    for o in range(n_ori):
-        terms[o] = brick[o * share:(o + 1) * share, :]
-
-    def term_copy(step, slot):
-        to = (ori + step) % n_ori
+        n = side // positions
+        wide_hi = jnp.concatenate([hi[p * n:(p + 1) * n, :] for p in range(positions)], axis=1)
+        wide_lo = jnp.concatenate([lo[p * n:(p + 1) * n, :] for p in range(positions)], axis=1)
+        brick = jnp.dot(wide_hi, w_v[...], preferred_element_type=jnp.float32)
+        brick += jnp.dot(wide_lo, w_v[...], preferred_element_type=jnp.float32)
+        for c in range(CORES):
+            terms[chip * CORES + c] = brick[c * share:(c + 1) * share, :]
+
+    def term_copy(to, slot):
         return pltpu.make_async_remote_copy(
             src_ref=terms.at[to],
             dst_ref=terms_buf.at[slot],
-            send_sem=a_send.at[step],
+            send_sem=a_send.at[to],
             recv_sem=a_recv.at[slot],
             device_id=(me, to),
             device_id_type=MESH,
         )
 
-    for step in range(1, n_ori):
-        term_copy(step, ori).start()
+    values(0)
+
+    def first_side(f, c):
+        values(f + 1)
+        collect(f, 1 - x_me)
+        return c
+
+    lax.fori_loop(0, n_img - 1, first_side, 0)
+    collect(n_img - 1, 1 - x_me)
+    w_copy.wait()
+    brick_terms(1 - x_me)
+    for c in range(CORES):
+        term_copy((1 - x_me) * CORES + c, ori).start()
+
+    def second_side(f, c):
+        collect(f, x_me)
+        return c
+
+    lax.fori_loop(0, n_img, second_side, 0)
+    brick_terms(x_me)
+    mate = x_me * CORES + 1 - core
+    term_copy(mate, ori).start()
     mine = terms[ori]
-    for step in range(1, n_ori):
-        slot = (ori + step) % n_ori
-        term_copy(step, slot).wait_recv()
+    term_copy(mate, mate).wait_recv()
+    mine += terms_buf[mate]
+    for c in range(CORES):
+        slot = (1 - x_me) * CORES + c
+        term_copy(slot, slot).wait_recv()
         mine += terms_buf[slot]
     for i in range(n_img):
         mid[i] = mine[i * lines:(i + 1) * lines, :]
@@ -451,6 +513,53 @@
 
     for step in range(1, n_img):
         mid_copy(step, me).start()
+    for step in range(1, n_img):
+        code_copy(step).wait_send()
+    for step in range(1, n_ori):
+        stat_copy(step, ori).wait_send()
+        term_copy((ori + step) % n_ori, ori).wait_send()
+    for h in range(PARTS):
+        own = refs.at[pl.ds(h * quarter, quarter), :]
+
+        @pl.when(has_up)
+        def _():
+            piece(own, me, h, up_sem, up).wait_send()
+
+        @pl.when(has_dn)
+        def _():
+            piece(own, me, h, dn_sem, dn).wait_send()
+
+        piece(own, me, h, y_sem, yn).wait_send()
+
+    @pl.when(zp > z)
+    def _():
+        for late_q in range(PARTS // 2, PARTS):
+            piece(held(late_sl, late_q), late_sl, late_q, up_sem, up).wait_send()
+
+    @pl.when(zp < z)
+    def _():
+        for late_q in range(PARTS // 2, PARTS):
+            piece(held(late_sl, late_q), late_sl, late_q, dn_sem, dn).wait_send()
+
+    def drain(s, carry):
+        r, q, k, sl, ok, go_up, go_dn, go_y = place(s)
+
+        @pl.when(go_up)
+        def _():
+            piece(held(sl, q), sl, q, up_sem, up).wait_send()
+
+        @pl.when(go_dn)
+        def _():
+            piece(held(sl, q), sl, q, dn_sem, dn).wait_send()
+
+        @pl.when(go_y)
+        def _():
+            piece(held(sl, q), sl, q, y_sem, yn).wait_send()
+
+        return carry
+
+    lax.fori_loop(0, steps, drain, 0)
+
     result = mid[me]
     for step in range(1, n_img):
         slot = (me + step) % n_img
@@ -459,54 +568,8 @@
             result += mid_buf[slot]
     sums_out[0] = result
     sums_out[1] = mid_buf[(me + n_img - 1) % n_img]
-
     for step in range(1, n_img):
-        code_copy(step).wait_send()
         mid_copy(step, me).wait_send()
-    for step in range(1, n_ori):
-        stat_copy(step, ori).wait_send()
-        term_copy(step, ori).wait_send()
-    for h in range(PARTS):
-        own = refs.at[pl.ds(h * quarter, quarter), :]
-
-        @pl.when(has_up)
-        def _():
-            piece(own, me, h, up_sem, up).wait_send()
-
-        @pl.when(has_dn)
-        def _():
-            piece(own, me, h, dn_sem, dn).wait_send()
-
-        piece(own, me, h, y_sem, yn).wait_send()
-
-    @pl.when(zp > z)
-    def _():
-        for late_q in range(PARTS // 2, PARTS):
-            piece(held(late_sl, late_q), late_sl, late_q, up_sem, up).wait_send()
-
-    @pl.when(zp < z)
-    def _():
-        for late_q in range(PARTS // 2, PARTS):
-            piece(held(late_sl, late_q), late_sl, late_q, dn_sem, dn).wait_send()
-
-    def drain(s, carry):
-        r, q, k, sl, ok, go_up, go_dn, go_y = place(s)
-
-        @pl.when(go_up)
-        def _():
-            piece(held(sl, q), sl, q, up_sem, up).wait_send()
-
-        @pl.when(go_dn)
-        def _():
-            piece(held(sl, q), sl, q, dn_sem, dn).wait_send()
-
-        @pl.when(go_y)
-        def _():
-            piece(held(sl, q), sl, q, y_sem, yn).wait_send()
-
-        return carry
-
-    lax.fori_loop(0, steps, drain, 0)
 
 
 def finish(sums, stats, bricks, evidence):
@@ -540,15 +603,14 @@
         scratch_shapes=[
             pltpu.VMEM((n_img, n_images, depth), bf16),
             pltpu.VMEM((n_img, rows, depth), bf16),
-            pltpu.VMEM((positions, tile_width, voxels), bf16),
+            pltpu.VMEM((positions * tile_width, voxels), bf16),
             pltpu.VMEM((n_images // LANES, rows, LANES), f32),
             pltpu.VMEM((rows, n_images), bf16),
-            pltpu.VMEM((tiles_ref // 2, LANES), i32),
-            pltpu.VMEM((n_img, tiles_ref // 2, LANES), i32),
+            pltpu.VMEM((tiles_ref // 4, LANES), i32),
+            pltpu.VMEM((n_img, tiles_ref // 4, LANES), i32),
             pltpu.VMEM((tiles_ref, rows), i32),
-            pltpu.VMEM((n_img, cells, rows * depth // tile_width), bf16),
-            pltpu.VMEM((rows * depth // tile_width, 2 * tile_width), bf16),
-            pltpu.VMEM((rows * depth // tile_width, 2 * tile_width), bf16),
+            pltpu.VMEM((n_img, cells, rows * depth // tile_width), F8),
+            pltpu.VMEM((n_img, rows * depth // tile_width, 2 * tile_width), F8),
             pltpu.VMEM((cells, 2 * tile_width), f32),
             pltpu.VMEM((4, n_images), f32),
             pltpu.VMEM((2, n_images), f32),
@@ -572,6 +634,7 @@
             dma((n_ori,)),
             dma((n_img,)),
             dma((n_img,)),
+            pltpu.SemaphoreType.REGULAR((n_img // NY - 1,)),
         ],
         compiler_params=pltpu.CompilerParams(
             collective_id=0, has_side_effects=True, vmem_limit_bytes=67043328
@@ -584,7 +647,7 @@
         tile_owner.reshape(flat),
         tile_brick.reshape(flat),
         tile_block.reshape(flat),
-        distance_weights,
+        distance_weights.reshape(positions * tile_width, voxels),
     )
     bricks, evidence = pl.pallas_call(
         finish,
@@ -609,6 +672,9 @@
         depth % LANES == 0
         and 2 * (rows // n_img) == LANES
         and LANES % tiles_ref == 0
+        and tiles_ref % 32 == 0
+        and cells <= PACK // 2
+        and lax.axis_size("ori") == 2 * CORES
         and rows * tiles_ref == 16 * LANES * n_img
         and n_img % (2 * NY) == 0
         and n_img >= 4 * NY

time: 83.5 us -> 78.2 us (0.937)
  Pallas kernels: 82.5 us -> 77.2 us
    pallas_call x1, Pallas kernels: 81.2 us -> 75.9 us  [fused_body(): pl.pallas_call(functools.partial(kernel, n_img, n_ori, tiles_ref, 1.0 / m...]
where the time goes in v1:
time: 78.2 us; the launch traced here: 77.8 us
  Pallas kernels  77.2 us (99%)
    pallas_call x1, Pallas kernels, fused_body(): pl.pallas_call(functools.partial(kernel, n_img, n_ori, tiles_ref, 1.0 / m...  75.9 us

profile of v1, /device:TPU:0, one launch (start us, length us, event | category | flops | bytes accessed | tf_op | source)
XLA Modules:
  0.0 77.8 jit_solution(3562134117165493312)
XLA Ops:
  0.6 75.9 %shard_map.95 = (f32[2,4,512]{2,1,0:T(4,128)}, f32[2,1024]{1,0:T(2,128)}) custom-call(bf16[512,512]{1,0:T(8,128)(2,1)} %refs.1, bf16[1024,4096]{1,0:T(8,128)(2,1)} %images.1, f32[1,1024]{1,0:T(1,128)} %bitcast.12, s32[2,1024]{1,0:T(2,128)} %bitcast.8, s32[16,128]{1,0:T(8,128)} %bitcast.9, s32[16,128]{1,0:T(8,128)} %bitcast.10, s32[16,128]{1,0:T(8,128)} %bitcast.11, ...), custom_call_target="tpu_custom_call" | custom-call | tf_op jit(solution)/shard_map/pallas_call | solution.py:595
  76.5 1.3 %shard_map.96 = (f32[4,512]{1,0:T(4,128)}, f32[1,1024]{1,0:T(1,128)}) custom-call(f32[2,4,512]{2,1,0:T(4,128)} %get-tuple-element.6.sums, f32[2,1024]{1,0:T(2,128)} %get-tuple-element.7.stats), custom_call_target="tpu_custom_call" | custom-call | tf_op jit(solution)/shard_map/pallas_call | solution.py:652

commit v2 on v1

--- a/solution.py
+++ b/solution.py
@@ -70,7 +70,7 @@
     n_img, n_ori, tiles_ref, inv_root,
     refs, images, scale, pattern, owner, brick_of, block_of, weights,
     sums_out, stats_out,
-    img_v, buf, w_v, sc, scaled, codes, codes_buf, codes_all, onehot, rhs, acc,
+    img_v, buf, w_v, sc, scaled, codes, codes_buf, codes_all, onehot, rhs_a, rhs_b, acc,
     halves, stats, stats_buf, terms, terms_buf, mid, mid_buf,
     img_sem, w_sem, own_sem, up_sem, dn_sem, y_sem, recv_sem, code_send, code_recv,
     stat_send, stat_recv, a_send, a_recv, b_send, b_recv, hop_sem,
@@ -96,13 +96,8 @@
             images.at[:, pl.ds(f * depth, depth)], img_v.at[f], img_sem.at[f]
         )
 
-    for f in range(n_img):
-        image_copy(f).start()
     w_copy = pltpu.make_async_copy(weights, w_v, w_sem)
-    w_copy.start()
-
     own_copy = pltpu.make_async_copy(refs, buf.at[me], own_sem)
-    own_copy.start()
 
     up, dn, yn = me + NY, me - NY, z * NY + 1 - y
     has_up, has_dn = z < nz - 1, z > 0
@@ -197,6 +192,10 @@
 
         piece(own, me, h, y_sem, yn).start()
 
+    own_copy.start()
+    for f in range(n_img):
+        image_copy(f).start()
+    w_copy.start()
     for hop in range(nz - 1):
         greet(hop_sem.at[hop])
         pl.semaphore_wait(hop_sem.at[hop], near)
@@ -409,7 +408,7 @@
     share_of = scale[...] / mass
 
     spread = LANES // tiles_ref
-    power = jnp.zeros((strip, 1), jnp.float32)
+    power = jnp.zeros((strip, LANES), jnp.float32)
     for h in range(2):
         weight = jnp.exp(halves[2 * h:2 * h + 1, :] - peak) * share_of
 
@@ -419,30 +418,35 @@
             at = pl.ds(pl.multiple_of(i * strip, strip), strip)
             value = score_rows(pl.ds(first, strip, stride=spread)) * weight
             scaled[at, :] = value.astype(jnp.bfloat16)
-            return jnp.maximum(top, jnp.sum(value * value, axis=1, keepdims=True))
+            square = value * value
+            held = square[:, 0:LANES]
+            for c in range(1, blocks):
+                held += square[:, c * LANES:(c + 1) * LANES]
+            return jnp.maximum(top, held)
 
         power = lax.fori_loop(0, n_strips, scale_of, power)
-    largest = jnp.maximum(jnp.sqrt(jnp.max(power, axis=0, keepdims=True)), 1e-15)
+    power = jnp.max(jnp.sum(power, axis=1, keepdims=True), axis=0, keepdims=True)
+    largest = jnp.maximum(jnp.sqrt(power), 1e-15)
     largest = largest * (math.sqrt(n_images) * jnp.maximum(bright, 1e-18))
     grow, shrink = TOP / largest, largest * (1.0 / TOP)
 
-    def values(f):
+    def values(f, j, rhs):
         value = jnp.dot(scaled[...], img_v[f], preferred_element_type=jnp.float32) * grow
         hi = value.astype(F8)
         lo = ((value - hi.astype(jnp.float32)) * LOW).astype(F8)
         for q in range(chunk_tiles):
             cut = slice(q * tile_width, (q + 1) * tile_width)
-            rhs[f, q * rows:(q + 1) * rows, 0:tile_width] = hi[:, cut]
-            rhs[f, q * rows:(q + 1) * rows, tile_width:] = lo[:, cut]
+            rhs[j, q * rows:(q + 1) * rows, 0:tile_width] = hi[:, cut]
+            rhs[j, q * rows:(q + 1) * rows, tile_width:] = lo[:, cut]
 
     x_me, core = ori // CORES, ori % CORES
     chips = n_ori // CORES
     side = cells // chips
     share = n_img * lines
 
-    def collect(f, chip):
+    def collect(f, j, rhs, chip):
         at = pl.ds(pl.multiple_of(chip * side, side), side)
-        acc[at, :] += jnp.dot(onehot[f, at, :], rhs[f], preferred_element_type=jnp.float32)
+        acc[at, :] += jnp.dot(onehot[f, at, :], rhs[j], preferred_element_type=jnp.float32)
 
     def brick_terms(chip):
         at = pl.ds(pl.multiple_of(chip * side, side), side)
@@ -468,25 +472,31 @@
             device_id_type=MESH,
         )
 
-    values(0)
-
-    def first_side(f, c):
-        values(f + 1)
-        collect(f, 1 - x_me)
+    values(0, 0, rhs_a)
+
+    def first_side(j, c):
+        values(2 * j + 1, j, rhs_b)
+        collect(2 * j, j, rhs_a, 1 - x_me)
+        values(2 * j + 2, j + 1, rhs_a)
+        collect(2 * j + 1, j, rhs_b, 1 - x_me)
         return c
 
-    lax.fori_loop(0, n_img - 1, first_side, 0)
-    collect(n_img - 1, 1 - x_me)
+    last = n_img // 2 - 1
+    lax.fori_loop(0, last, first_side, 0)
+    values(n_img - 1, last, rhs_b)
+    collect(n_img - 2, last, rhs_a, 1 - x_me)
+    collect(n_img - 1, last, rhs_b, 1 - x_me)
     w_copy.wait()
     brick_terms(1 - x_me)
     for c in range(CORES):
         term_copy((1 - x_me) * CORES + c, ori).start()
 
-    def second_side(f, c):
-        collect(f, x_me)
+    def second_side(j, c):
+        collect(2 * j, j, rhs_a, x_me)
+        collect(2 * j + 1, j, rhs_b, x_me)
         return c
 
-    lax.fori_loop(0, n_img, second_side, 0)
+    lax.fori_loop(0, n_img // 2, second_side, 0)
     brick_terms(x_me)
     mate = x_me * CORES + 1 - core
     term_copy(mate, ori).start()
@@ -610,7 +620,8 @@
             pltpu.VMEM((n_img, tiles_ref // 4, LANES), i32),
             pltpu.VMEM((tiles_ref, rows), i32),
             pltpu.VMEM((n_img, cells, rows * depth // tile_width), F8),
-            pltpu.VMEM((n_img, rows * depth // tile_width, 2 * tile_width), F8),
+            pltpu.VMEM((n_img // 2, rows * depth // tile_width, 2 * tile_width), F8),
+            pltpu.VMEM((n_img // 2, rows * depth // tile_width, 2 * tile_width), F8),
             pltpu.VMEM((cells, 2 * tile_width), f32),
             pltpu.VMEM((4, n_images), f32),
             pltpu.VMEM((2, n_images), f32),

time: 78.2 us -> 74.8 us (0.957)
  Pallas kernels: 77.2 us -> 73.9 us
    pallas_call x1, Pallas kernels: 75.9 us -> 72.5 us  [fused_body(): pl.pallas_call(functools.partial(kernel, n_img, n_ori, tiles_ref, 1.0 / m...]
where the time goes in v2:
time: 74.8 us; the launch traced here: 74.5 us
  Pallas kernels  73.9 us (99%)
    pallas_call x1, Pallas kernels, fused_body(): pl.pallas_call(functools.partial(kernel, n_img, n_ori, tiles_ref, 1.0 / m...  72.5 us

profile of v2, /device:TPU:0, one launch (start us, length us, event | category | flops | bytes accessed | tf_op | source)
XLA Modules:
  0.0 74.5 jit_solution(7320417541446177856)
XLA Ops:
  0.6 72.5 %shard_map.95 = (f32[2,4,512]{2,1,0:T(4,128)}, f32[2,1024]{1,0:T(2,128)}) custom-call(bf16[512,512]{1,0:T(8,128)(2,1)} %refs.1, bf16[1024,4096]{1,0:T(8,128)(2,1)} %images.1, f32[1,1024]{1,0:T(1,128)} %bitcast.12, s32[2,1024]{1,0:T(2,128)} %bitcast.8, s32[16,128]{1,0:T(8,128)} %bitcast.9, s32[16,128]{1,0:T(8,128)} %bitcast.10, s32[16,128]{1,0:T(8,128)} %bitcast.11, ...), custom_call_target="tpu_custom_call" | custom-call | tf_op jit(solution)/shard_map/pallas_call | solution.py:605
  73.2 1.3 %shard_map.96 = (f32[4,512]{1,0:T(4,128)}, f32[1,1024]{1,0:T(1,128)}) custom-call(f32[2,4,512]{2,1,0:T(4,128)} %get-tuple-element.6.sums, f32[2,1024]{1,0:T(2,128)} %get-tuple-element.7.stats), custom_call_target="tpu_custom_call" | custom-call | tf_op jit(solution)/shard_map/pallas_call | solution.py:663

commit v3 on v2

--- a/solution.py
+++ b/solution.py
@@ -457,8 +457,9 @@
         n = side // positions
         wide_hi = jnp.concatenate([hi[p * n:(p + 1) * n, :] for p in range(positions)], axis=1)
         wide_lo = jnp.concatenate([lo[p * n:(p + 1) * n, :] for p in range(positions)], axis=1)
-        brick = jnp.dot(wide_hi, w_v[...], preferred_element_type=jnp.float32)
-        brick += jnp.dot(wide_lo, w_v[...], preferred_element_type=jnp.float32)
+        wide = jnp.concatenate([wide_hi, wide_lo], axis=0)
+        brick = jnp.dot(wide, w_v[...], preferred_element_type=jnp.float32)
+        brick = brick[0:n, :] + brick[n:, :]
         for c in range(CORES):
             terms[chip * CORES + c] = brick[c * share:(c + 1) * share, :]
 

time: 74.8 us -> 74.4 us (level)
  no operation moved by 1% of the time
where the time goes in v3:
time: 74.4 us; the launch traced here: 74.1 us
  Pallas kernels  73.4 us (99%)
    pallas_call x1, Pallas kernels, fused_body(): pl.pallas_call(functools.partial(kernel, n_img, n_ori, tiles_ref, 1.0 / m...  72.1 us

profile of v3, /device:TPU:0, one launch (start us, length us, event | category | flops | bytes accessed | tf_op | source)
XLA Modules:
  0.0 74.1 jit_solution(9140815076793595076)
XLA Ops:
  0.6 72.1 %shard_map.95 = (f32[2,4,512]{2,1,0:T(4,128)}, f32[2,1024]{1,0:T(2,128)}) custom-call(bf16[512,512]{1,0:T(8,128)(2,1)} %refs.1, bf16[1024,4096]{1,0:T(8,128)(2,1)} %images.1, f32[1,1024]{1,0:T(1,128)} %bitcast.12, s32[2,1024]{1,0:T(2,128)} %bitcast.8, s32[16,128]{1,0:T(8,128)} %bitcast.9, s32[16,128]{1,0:T(8,128)} %bitcast.10, s32[16,128]{1,0:T(8,128)} %bitcast.11, ...), custom_call_target="tpu_custom_call" | custom-call | tf_op jit(solution)/shard_map/pallas_call | solution.py:606
  72.7 1.3 %shard_map.96 = (f32[4,512]{1,0:T(4,128)}, f32[1,1024]{1,0:T(1,128)}) custom-call(f32[2,4,512]{2,1,0:T(4,128)} %get-tuple-element.6.sums, f32[2,1024]{1,0:T(2,128)} %get-tuple-element.7.stats), custom_call_target="tpu_custom_call" | custom-call | tf_op jit(solution)/shard_map/pallas_call | solution.py:664

commit v4 on v3

--- a/solution.py
+++ b/solution.py
@@ -288,7 +288,7 @@
             return jnp.maximum(m, s)
 
         m = lax.fori_loop(
-            0, n_strips, peak_of, jnp.full((strip, n_images), -1e30, jnp.float32)
+            0, n_strips, peak_of, jnp.full((strip, n_images), -1e30, jnp.float32), unroll=2
         )
         m = jnp.max(m, axis=0, keepdims=True)
 
@@ -298,7 +298,9 @@
             keep_rows(at, e)
             return t + e
 
-        t = lax.fori_loop(0, n_strips, mass_of, jnp.zeros((strip, n_images), jnp.float32))
+        t = lax.fori_loop(
+            0, n_strips, mass_of, jnp.zeros((strip, n_images), jnp.float32), unroll=2
+        )
         halves[2 * h:2 * h + 1, :] = m
         halves[2 * h + 1:2 * h + 2, :] = jnp.sum(t, axis=0, keepdims=True)
 
@@ -424,7 +426,7 @@
                 held += square[:, c * LANES:(c + 1) * LANES]
             return jnp.maximum(top, held)
 
-        power = lax.fori_loop(0, n_strips, scale_of, power)
+        power = lax.fori_loop(0, n_strips, scale_of, power, unroll=2)
     power = jnp.max(jnp.sum(power, axis=1, keepdims=True), axis=0, keepdims=True)
     largest = jnp.maximum(jnp.sqrt(power), 1e-15)
     largest = largest * (math.sqrt(n_images) * jnp.maximum(bright, 1e-18))

time: 74.4 us -> 73.9 us (level)
  no operation moved by 1% of the time
where the time goes in v4:
time: 73.9 us; the launch traced here: 73.5 us
  Pallas kernels  72.9 us (99%)
    pallas_call x1, Pallas kernels, fused_body(): pl.pallas_call(functools.partial(kernel, n_img, n_ori, tiles_ref, 1.0 / m...  71.6 us

profile of v4, /device:TPU:0, one launch (start us, length us, event | category | flops | bytes accessed | tf_op | source)
XLA Modules:
  0.0 73.5 jit_solution(16153543959646635625)
XLA Ops:
  0.6 71.6 %shard_map.95 = (f32[2,4,512]{2,1,0:T(4,128)}, f32[2,1024]{1,0:T(2,128)}) custom-call(bf16[512,512]{1,0:T(8,128)(2,1)} %refs.1, bf16[1024,4096]{1,0:T(8,128)(2,1)} %images.1, f32[1,1024]{1,0:T(1,128)} %bitcast.12, s32[2,1024]{1,0:T(2,128)} %bitcast.8, s32[16,128]{1,0:T(8,128)} %bitcast.9, s32[16,128]{1,0:T(8,128)} %bitcast.10, s32[16,128]{1,0:T(8,128)} %bitcast.11, ...), custom_call_target="tpu_custom_call" | custom-call | tf_op jit(solution)/shard_map/pallas_call | solution.py:608
  72.2 1.3 %shard_map.96 = (f32[4,512]{1,0:T(4,128)}, f32[1,1024]{1,0:T(1,128)}) custom-call(f32[2,4,512]{2,1,0:T(4,128)} %get-tuple-element.6.sums, f32[2,1024]{1,0:T(2,128)} %get-tuple-element.7.stats), custom_call_target="tpu_custom_call" | custom-call | tf_op jit(solution)/shard_map/pallas_call | solution.py:666
